TPU v7x, 32 devices: a whole 2x2x4 slice. The times are simulated.
32 devices in a mesh: chaos: 4 (over z), gx: 4 (over y, x), gy: 2 (over core).
Axes of the slice: x: 2, y: 2, z: 4, core: 2. Of those that a mesh axis runs over, the one named last changes fastest.
Arguments:
- lam_start: float32 [286, 16, 512], P(None, ('chaos', 'gy'), 'gx'), may hold values from -6 to 6
- adj_source: float32 [286, 16, 512], P(None, ('chaos', 'gy'), 'gx'), may hold values from -6 to 6
- coef_points: float32 [512, 4, 4, 512], P('chaos', None, 'gy', 'gx'), may hold values from 0.1 to 1
- quad_index: int32 [512, 10], replicated, may hold values from 0 to 3
- mode_index: int32 [286, 10], replicated, may hold values from 0 to 3, as said below
Outputs:
- lam_end: float32 [286, 16, 512], P(None, ('chaos', 'gy'), 'gx')
Inputs may be any that keep to these rules, and one draw needn't show every extreme that they name: `mode_index`: each row is a multi-index whose degrees sum to at most 3; each such multi-index of 10 inputs appears exactly once.
All inputs are finite; a program needn't handle non-finite values.
Results may differ from a plain program's by a relative error of at most 0.00011.
Values sent between devices are 32-bit elements; how exact they have to be, the bound alone decides.
A program may use at most 64 MiB of HBM per device.

v0:
```python
import math
import jax
import jax.numpy as jnp
from jax import lax
from jax.sharding import PartitionSpec as P

STEPS = 2
gauss_nodes = (-2.3344142183389773, -0.7419637843027259, 0.7419637843027259, 2.3344142183389773)
gauss_weights = (0.04587585476806849, 0.4541241452319315, 0.4541241452319315, 0.04587585476806849)
mass_shift = 1.0
relax_rate = 0.2
top_prec = lax.Precision.HIGHEST


def tables(quad_index, mode_index):
    node_vals = jnp.array(gauss_nodes, jnp.float32)
    node_wts = jnp.array(gauss_weights, jnp.float32)
    hermite = jnp.stack(
        [
            jnp.ones_like(node_vals),
            node_vals,
            (node_vals * node_vals - 1.0) / math.sqrt(2.0),
            (node_vals * node_vals * node_vals - 3.0 * node_vals) / math.sqrt(6.0),
        ],
        0,
    )
    levels = jnp.arange(4, dtype=jnp.int32)
    quad_hot = (quad_index[:, :, None] == levels[None, None, :]).astype(jnp.float32)
    mode_hot = (mode_index[:, :, None] == levels[None, None, :]).astype(jnp.float32)
    at_nodes = jnp.einsum("qdk,nk->qdn", quad_hot, hermite, precision=top_prec)
    factors = jnp.einsum("qdn,pdn->qpd", at_nodes, mode_hot, precision=top_prec)
    chaos_basis = jnp.prod(factors, axis=2)
    point_wts = jnp.prod(jnp.sum(quad_hot * node_wts[None, None, :], axis=2), axis=1)
    point_wts = point_wts / jnp.sum(point_wts)
    back_map = chaos_basis * point_wts[:, None]
    return (chaos_basis, back_map)


def shift_pair(low, high, axis):
    size = lax.axis_size(axis)
    up = [(i, (i + 1) % size) for i in range(size)]
    down = [(j, i) for i, j in up]
    return (lax.ppermute(high, axis, up), lax.ppermute(low, axis, down))


def local(lam_start, adj_source, coef_points, quad_index, mode_index):
    modes, row_len, col_len = lam_start.shape
    points = quad_index.shape[0]
    rows = ("chaos", "gy")
    row_dev = lax.axis_index(rows)
    row_devs = lax.axis_size(rows)
    keep_low = jnp.where(row_dev == 0, 0.0, 1.0).astype(jnp.float32)
    keep_high = jnp.where(row_dev == row_devs - 1, 0.0, 1.0).astype(jnp.float32)
    coef = lax.all_to_all(coef_points, "chaos", split_axis=1, concat_axis=0, tiled=True)
    coef = coef.reshape(points, row_len, col_len)
    k_low, k_high = shift_pair(coef[:, 0], coef[:, -1], rows)
    k_left, k_right = shift_pair(coef[:, :, :1], coef[:, :, -1:], "gx")
    chaos_basis, back_map = tables(quad_index, mode_index)
    coef_y = [k_low * keep_low] + [coef[:, r] for r in range(row_len)] + [k_high * keep_high]
    coef_x = [jnp.concatenate([k_left[:, r], coef[:, r], k_right[:, r]], 1) for r in range(row_len)]
    lam_now = lam_start
    for repeat in range(STEPS):
        v_low, v_high = shift_pair(lam_now[:, :2], lam_now[:, -2:], rows)
        v_left, v_right = shift_pair(lam_now[:, :, :2], lam_now[:, :, -2:], "gx")
        v_low = v_low * keep_low
        v_high = v_high * keep_high
        parts = (
            [v_low[:, 0], v_low[:, 1]]
            + [lam_now[:, r] for r in range(row_len)]
            + [v_high[:, 0], v_high[:, 1]]
        )
        edges = [v_left[:, r] for r in range(row_len)] + [v_right[:, r] for r in range(row_len)]
        u = jnp.dot(
            chaos_basis,
            jnp.concatenate(parts + edges, 1),
            precision=top_prec,
            preferred_element_type=jnp.float32,
        )
        u_row = [u[:, i * col_len : (i + 1) * col_len] for i in range(row_len + 4)]
        base = (row_len + 4) * col_len
        u_left = [u[:, base + 2 * r : base + 2 * r + 2] for r in range(row_len)]
        base += 2 * row_len
        u_right = [u[:, base + 2 * r : base + 2 * r + 2] for r in range(row_len)]
        flux_y = [coef_y[i] * ((u_row[i + 2] - u_row[i]) * 0.5) for i in range(row_len + 2)]
        div = []
        for r in range(row_len):
            wide = jnp.concatenate([u_left[r], u_row[r + 2], u_right[r]], 1)
            flux_x = coef_x[r] * ((wide[:, 2:] - wide[:, :-2]) * 0.5)
            div.append((flux_x[:, 2:] - flux_x[:, :-2]) * 0.5 + (flux_y[r + 2] - flux_y[r]) * 0.5)
        back = jnp.dot(
            back_map.T,
            jnp.concatenate(div, 1),
            precision=top_prec,
            preferred_element_type=jnp.float32,
        )
        divergence = back.reshape(modes, row_len, col_len)
        lam_now = lam_now + relax_rate * (adj_source - (mass_shift * lam_now - divergence))
    return lam_now


def solution(mesh):
    placed = (
        P(None, ("chaos", "gy"), "gx"),
        P(None, ("chaos", "gy"), "gx"),
        P("chaos", None, "gy", "gx"),
        P(),
        P(),
    )
    return jax.shard_map(
        local, mesh=mesh, in_specs=placed, out_specs=P(None, ("chaos", "gy"), "gx"), check_vma=False
    )
```

profile of v0, /device:TPU:0, one launch (start us, length us, event | category | flops | bytes accessed | tf_op | source)
XLA Modules:
  0.0 80.5 jit_solution(6977557665041020564)
XLA Ops:
  0.0 1.0 %copy.78 = f32[286,2,128]{2,0,1:T(8,128)S(1)} copy(f32[286,2,128]{2,1,0:T(2,128)} %param.7) | data formatting | bytes 585728 | tf_op args[0]
  1.0 4.5 %collective-permute-start.3 = (f32[286,2,128]{2,0,1:T(8,128)S(1)}, f32[286,2,128]{2,0,1:T(8,128)S(1)}, u32[]{:S(2)}, u32[]{:S(2)}) collective-permute-start(f32[286,2,128]{2,0,1:T(8,128)S(1)} %copy.78), channel_id=1, source_target_pairs={{1,0},{8,1},{9,8},{16,9},{17,16},{24,17},{25,24},{0,25},{3,2},{10,... | collective-permute-start | bytes 878600 | tf_op jit(solution)/shard_map/ppermute | solution.py:43
  5.5 0.0 collective-permute-start.2
  5.5 2.0 %copy.67 = f32[128,4,2,128]{3,2,0,1:T(2,128)} copy(f32[128,4,2,128]{3,2,1,0:T(2,128)} %param.9) | data formatting | bytes 1048576 | tf_op args[2]
  7.6 3.6 %all-to-all-start = ((f32[128,4,2,128]{3,2,0,1:T(2,128)}), f32[128,4,2,128]{3,2,0,1:T(2,128)S(1)}, u32[]{:S(2)}, u32[]{:S(2)}) async-start(f32[128,4,2,128]{3,2,0,1:T(2,128)} %copy.67), calls=%async_computation | async-start | bytes 1048576 | tf_op jit(solution)/shard_map/all_to_all | solution.py:54
  11.2 0.1 fusion.64
  11.3 2.5 %collective-permute-start.5 = (f32[286,2,2]{2,0,1:T(8,128)S(1)}, f32[286,2,2]{2,0,1:T(8,128)S(1)}, u32[]{:S(2)}, u32[]{:S(2)}) collective-permute-start(f32[286,2,2]{2,0,1:T(8,128)S(1)} %get-tuple-element.35), channel_id=1, source_target_pairs={{2,0},{4,2},{6,4},{0,6},{3,1},{5,3},{7,5},{1,7},{10,8},{12,10},{14... | collective-permute-start | bytes 13736 | tf_op jit(solution)/shard_map/ppermute | solution.py:43
  13.8 0.0 collective-permute-start.4
  13.9 0.1 select_reduce_fusion
  14.0 0.6 reduce_sum.19
  14.6 1.2 %broadcast_divide_fusion = f32[512]{0:T(512)} fusion(f32[512]{0:T(512)S(1)} %reduce_prod.19, f32[]{:T(128)} %reduce_sum.19), kind=kLoop, calls=%fused_computation.109 | loop fusion | flops 512 | bytes 4100 | tf_op jit(solution)/shard_map/div | solution.py:34
  15.9 0.2 fusion.54
  16.1 3.4 %convolution_reduce_fusion = f32[286,512]{1,0:T(8,128)S(1)} fusion(f32[512,10,4]{0,2,1:T(4,128)S(1)} %fusion.54, s32[286,10]{0,1:T(8,128)} %param.11), kind=kOutput, calls=%fused_computation | convolution fusion | flops 71616688 | bytes 679088 | tf_op jit(solution)/shard_map/qdn,pdn->qpd/dot_general | solution.py:31
  19.5 1.4 %collective-permute-done.5 = f32[286,2,2]{2,0,1:T(8,128)S(1)} collective-permute-done((f32[286,2,2]{2,0,1:T(8,128)S(1)}, f32[286,2,2]{2,0,1:T(8,128)S(1)}, u32[]{:S(2)}, u32[]{:S(2)}) %collective-permute-start.5) | collective-permute-done | bytes 4608 | tf_op jit(solution)/shard_map/ppermute | solution.py:43
  20.9 7.3 %collective-permute-done.4 = f32[286,2,2]{2,0,1:T(8,128)S(1)} collective-permute-done((f32[286,2,2]{2,0,1:T(8,128)S(1)}, f32[286,2,2]{2,0,1:T(8,128)S(1)}, u32[]{:S(2)}, u32[]{:S(2)}) %collective-permute-start.4) | collective-permute-done | bytes 4608 | tf_op jit(solution)/shard_map/ppermute | solution.py:43
  28.2 0.0 collective-permute-done.3
  28.2 0.0 collective-permute-done.2
  28.3 1.2 %concatenate.47 = f32[286,776]{1,0:T(8,128)} concatenate(f32[286,128]{1,0:T(8,128)S(1)} %get-tuple-element.44, f32[286,128]{1,0:T(8,128)S(1)} %get-tuple-element.43, f32[286,128]{1,0:T(8,128)S(1)} %get-tuple-element.42, f32[286,128]{1,0:T(8,128)S(1)} %get-tuple-element.41, f32[286,128]{1,0:T(8,128)S(1)} %get-tuple-element.40, f32[286,128]{1,0:T(8,128)S(1)} %get-tuple-element.39, ...), dimensions={1} | concatenate | bytes 1775488 | tf_op jit(solution)/shard_map/concatenate | solution.py:75
  29.5 3.9 %fusion.65 = f32[512,776]{0,1:T(8,128)S(1)} fusion(f32[286,512]{1,0:T(8,128)S(1)} %convolution_reduce_fusion, f32[286,776]{1,0:T(8,128)} %concatenate.47), kind=kOutput, calls=%fused_computation.118 | convolution fusion | flops 1363574784 | bytes 3062720 | tf_op jit(solution)/shard_map/dot_general | solution.py:73
  33.5 0.0 all-to-all-done
  33.5 1.4 %fusion.62 = (f32[512,2,1]{2,1,0:T(2,128)S(1)}, f32[512,2,1]{2,1,0:T(2,128)}) fusion(f32[512,2,128]{2,1,0:T(2,128)S(1)} %bitcast.66), kind=kLoop, calls=%fused_computation.115 | loop fusion | bytes 16384 | tf_op jit(solution)/shard_map/slice | solution.py:57
  34.9 1.2 %copy.97 = f32[512,2,1]{0,2,1:T(1,128)S(1)} copy(f32[512,2,1]{2,1,0:T(2,128)} %get-tuple-element.20) | data formatting | bytes 8192
  36.1 1.5 %collective-permute-start.1 = (f32[512,2,1]{0,2,1:T(1,128)S(1)}, f32[512,2,1]{0,2,1:T(1,128)S(1)}, u32[]{:S(2)}, u32[]{:S(2)}) collective-permute-start(f32[512,2,1]{0,2,1:T(1,128)S(1)} %copy.97), channel_id=1, source_target_pairs={{2,0},{4,2},{6,4},{0,6},{3,1},{5,3},{7,5},{1,7},{10,8},{12,10},{14... | collective-permute-start | bytes 12296 | tf_op jit(solution)/shard_map/ppermute | solution.py:43
  37.6 1.2 %fusion.61 = (f32[512,1,128]{2,1,0:T(1,128)}, f32[512,1,128]{2,1,0:T(1,128)}) fusion(f32[512,2,128]{2,1,0:T(2,128)S(1)} %bitcast.67), kind=kLoop, calls=%fused_computation.114 | loop fusion | bytes 1048576 | tf_op jit(solution)/shard_map/slice | solution.py:60
  38.7 1.1 %copy.96 = f32[512,1,128]{0,2,1:T(8,128)S(1)} copy(f32[512,1,128]{2,1,0:T(1,128)} %get-tuple-element.17) | data formatting | bytes 524288
  39.8 1.1 %copy.98 = f32[512,1,128]{0,2,1:T(8,128)S(1)} copy(f32[512,1,128]{2,1,0:T(1,128)} %get-tuple-element.18) | data formatting | bytes 524288
  40.9 0.1 collective-permute-start.6
  41.0 3.5 %collective-permute-start.7 = (f32[512,128]{0,1:T(8,128)S(1)}, f32[512,128]{0,1:T(8,128)}, u32[]{:S(2)}, u32[]{:S(2)}) collective-permute-start(f32[512,128]{0,1:T(8,128)S(1)} %bitcast.68), channel_id=1, source_target_pairs={{1,0},{8,1},{9,8},{16,9},{17,16},{24,17},{25,24},{0,25},{3,2},{10,... | collective-permute-start | bytes 786440 | tf_op jit(solution)/shard_map/ppermute | solution.py:43
  44.5 0.2 copy.95
  44.7 0.6 collective-permute-start
  45.3 0.0 collective-permute-done.1
  45.3 3.9 %collective-permute-done = f32[512,2,1]{0,2,1:T(1,128)S(1)} collective-permute-done((f32[512,2,1]{0,2,1:T(1,128)S(1)}, f32[512,2,1]{0,2,1:T(1,128)S(1)}, u32[]{:S(2)}, u32[]{:S(2)}) %collective-permute-start) | collective-permute-done | bytes 4128 | tf_op jit(solution)/shard_map/ppermute | solution.py:43
  49.2 0.1 fusion.19
  49.3 0.5 copy-done.13
  49.8 0.0 collective-permute-done.6
  49.8 1.1 %fusion.51 = (f32[512,128]{0,1:T(8,128)S(1)}, f32[512,128]{0,1:T(8,128)S(1)}) fusion(f32[512,776]{0,1:T(8,128)S(1)} %copy-done.1, f32[512,130]{0,1:T(8,128)S(1)} %fusion.19, f32[512,128]{0,1:T(8,128)} %collective-permute-done.6, f32[]{:T(128)S(6)} %select_n.7, f32[512,1,128]{0,2,1:T(8,128)S(1)} %copy.98), kind=kLoop, calls=%fused_computation.70 | loop fusion | flops 720896 | bytes 2621444 | tf_op jit(solution)/shard_map/add | solution.py:89
  51.0 0.1 fusion.21
  51.1 0.0 copy-start.2
  51.1 0.0 copy-start.3
  51.1 0.0 collective-permute-done.7
  51.1 1.2 %fusion.44 = f32[512,128]{0,1:T(8,128)S(1)} fusion(f32[512,776]{0,1:T(8,128)S(1)} %copy-done.1, f32[512,130]{0,1:T(8,128)S(1)} %fusion.21, f32[512,128]{0,1:T(8,128)} %collective-permute-done.7, f32[]{:T(128)S(6)} %select_n.8, f32[512,1,128]{0,2,1:T(8,128)S(1)} %copy.96), kind=kLoop, calls=%fused_computation.60 | loop fusion | flops 720896 | bytes 2097156 | tf_op jit(solution)/shard_map/add | solution.py:89
  52.3 0.7 fusion.2
  53.0 0.2 reshape.17
  53.2 0.1 fusion.15
  53.3 0.1 fusion.63
  53.4 0.1 collective-permute-start.11
  53.5 2.1 %collective-permute-start.9 = (f32[286,2,128]{2,0,1:T(8,128)S(1)}, f32[286,2,128]{2,0,1:T(8,128)S(1)}, u32[]{:S(2)}, u32[]{:S(2)}) collective-permute-start(f32[286,2,128]{2,0,1:T(8,128)S(1)} %fusion.15), channel_id=1, source_target_pairs={{1,0},{8,1},{9,8},{16,9},{17,16},{24,17},{25,24},{0,25},{3,2},{10,... | collective-permute-start | bytes 878600 | tf_op jit(solution)/shard_map/ppermute | solution.py:43
  55.7 1.5 %collective-permute-start.10 = (f32[286,2,2]{2,0,1:T(8,128)S(1)}, f32[286,2,2]{2,0,1:T(8,128)S(1)}, u32[]{:S(2)}, u32[]{:S(2)}) collective-permute-start(f32[286,2,2]{2,0,1:T(8,128)S(1)} %get-tuple-element.24), channel_id=1, source_target_pairs={{0,2},{2,4},{4,6},{6,0},{1,3},{3,5},{5,7},{7,1},{8,10},{10,12},{12... | collective-permute-start | bytes 13736 | tf_op jit(solution)/shard_map/ppermute | solution.py:43
  57.2 6.2 %collective-permute-done.11 = f32[286,2,2]{2,0,1:T(8,128)S(1)} collective-permute-done((f32[286,2,2]{2,0,1:T(8,128)S(1)}, f32[286,2,2]{2,0,1:T(8,128)S(1)}, u32[]{:S(2)}, u32[]{:S(2)}) %collective-permute-start.11) | collective-permute-done | bytes 4608 | tf_op jit(solution)/shard_map/ppermute | solution.py:43
  63.3 6.4 %collective-permute-done.10 = f32[286,2,2]{2,0,1:T(8,128)S(1)} collective-permute-done((f32[286,2,2]{2,0,1:T(8,128)S(1)}, f32[286,2,2]{2,0,1:T(8,128)S(1)}, u32[]{:S(2)}, u32[]{:S(2)}) %collective-permute-start.10) | collective-permute-done | bytes 4608 | tf_op jit(solution)/shard_map/ppermute | solution.py:43
  69.8 0.7 slice_bitcast_fusion.2
  70.4 0.0 collective-permute-done.9
  70.5 0.7 slice_bitcast_fusion.4
  71.2 0.7 slice_bitcast_fusion.8
  71.9 1.4 %concatenate.54 = f32[286,776]{1,0:T(8,128)S(1)} concatenate(f32[286,128]{1,0:T(8,128)} %get-tuple-element.32, f32[286,128]{1,0:T(8,128)} %get-tuple-element.31, f32[286,128]{1,0:T(8,128)S(1)} %get-tuple-element.30, f32[286,128]{1,0:T(8,128)S(1)} %get-tuple-element.29, f32[286,128]{1,0:T(8,128)} %get-tuple-element.28, f32[286,128]{1,0:T(8,128)} %get-tuple-element.27, ...), dimensions={1} | concatenate | bytes 1775488 | tf_op jit(solution)/shard_map/concatenate | solution.py:75
  73.3 2.7 %fusion.66 = f32[512,776]{0,1:T(8,128)S(1)} fusion(f32[286,512]{1,0:T(8,128)S(1)} %convolution_reduce_fusion, f32[286,776]{1,0:T(8,128)S(1)} %concatenate.54), kind=kOutput, calls=%fused_computation.119 | convolution fusion | flops 1363574784 | bytes 3062720 | tf_op jit(solution)/shard_map/dot_general | solution.py:73
  76.1 0.1 fusion.23
  76.2 1.1 %fusion.37 = (f32[512,128]{0,1:T(8,128)S(1)}, f32[512,128]{0,1:T(8,128)S(1)}) fusion(f32[512,776]{0,1:T(8,128)S(1)} %fusion.66, f32[512,130]{0,1:T(8,128)S(1)} %fusion.23, f32[512,128]{0,1:T(8,128)} %collective-permute-done.6, f32[]{:T(128)S(6)} %select_n.7, f32[512,1,128]{0,2,1:T(8,128)S(1)} %copy.98), kind=kLoop, calls=%fused_computation.50 | loop fusion | flops 720896 | bytes 2621444 | tf_op jit(solution)/shard_map/add | solution.py:89
  77.4 0.1 fusion.25
  77.5 1.1 %fusion.30 = f32[512,128]{0,1:T(8,128)S(1)} fusion(f32[512,776]{0,1:T(8,128)S(1)} %fusion.66, f32[512,130]{0,1:T(8,128)S(1)} %fusion.25, f32[512,128]{0,1:T(8,128)} %collective-permute-done.7, f32[]{:T(128)S(6)} %select_n.8, f32[512,1,128]{0,2,1:T(8,128)S(1)} %copy.96), kind=kLoop, calls=%fused_computation.40 | loop fusion | flops 720896 | bytes 2097156 | tf_op jit(solution)/shard_map/add | solution.py:89
  78.6 0.7 fusion
  79.3 0.2 reshape.18
  79.5 0.1 fusion.12
  79.5 0.9 %copy.89 = f32[286,2,128]{2,1,0:T(2,128)} copy(f32[286,2,128]{2,0,1:T(8,128)S(1)} %fusion.12) | data formatting | bytes 585728 | tf_op jit(solution)/shard_map/add | solution.py:97
  (52 shorter events, 0.4 us)
Async XLA Ops:
  1.0 27.2 %collective-permute-start.3 = (f32[286,2,128]{2,0,1:T(8,128)S(1)}, f32[286,2,128]{2,0,1:T(8,128)S(1)}, u32[]{:S(2)}, u32[]{:S(2)}) collective-permute-start(f32[286,2,128]{2,0,1:T(8,128)S(1)} %copy.78), channel_id=1, source_target_pairs={{1,0},{8,1},{9,8},{16,9},{17,16},{24,17},{25,24},{0,25},{3,2},{10,... | collective-permute-start | bytes 878600 | tf_op jit(solution)/shard_map/ppermute | solution.py:43
  5.5 22.7 %collective-permute-start.2 = (f32[286,2,128]{2,0,1:T(8,128)S(1)}, f32[286,2,128]{2,0,1:T(8,128)S(1)}, u32[]{:S(2)}, u32[]{:S(2)}) collective-permute-start(f32[286,2,128]{2,0,1:T(8,128)S(1)} %copy.78), channel_id=1, source_target_pairs={{0,1},{1,8},{8,9},{9,16},{16,17},{17,24},{24,25},{25,0},{2,3},{3,1... | collective-permute-start | bytes 878600 | tf_op jit(solution)/shard_map/ppermute | solution.py:43
  7.6 6.3 %copy-start.4 = (s32[512,10]{0,1:T(8,128)S(1)}, s32[512,10]{0,1:T(8,128)}, u32[]{:S(2)}) copy-start(s32[512,10]{0,1:T(8,128)} %param.10) | copy-start | bytes 61444
  7.6 6.3 %copy-start.16 = (f32[4]{0:T(128)S(1)}, f32[4]{0:T(128)}, u32[]{:S(2)}) copy-start(f32[4]{0:T(128)} %constant.42.clone) | copy-start | bytes 52
  7.6 8.3 %copy-start.15 = (f32[4,4,1]{1,0,2:T(4,128)S(1)}, f32[4,4,1]{1,0,2:T(4,128)}, u32[]{:S(2)}) copy-start(f32[4,4,1]{1,0,2:T(4,128)} %constant.56) | copy-start | bytes 196
  7.6 25.9 %all-to-all-start = ((f32[128,4,2,128]{3,2,0,1:T(2,128)}), f32[128,4,2,128]{3,2,0,1:T(2,128)S(1)}, u32[]{:S(2)}, u32[]{:S(2)}) async-start(f32[128,4,2,128]{3,2,0,1:T(2,128)} %copy.67), calls=%async_computation | async-start | bytes 1048576 | tf_op jit(solution)/shard_map/all_to_all | solution.py:54
  11.3 9.5 %collective-permute-start.5 = (f32[286,2,2]{2,0,1:T(8,128)S(1)}, f32[286,2,2]{2,0,1:T(8,128)S(1)}, u32[]{:S(2)}, u32[]{:S(2)}) collective-permute-start(f32[286,2,2]{2,0,1:T(8,128)S(1)} %get-tuple-element.35), channel_id=1, source_target_pairs={{2,0},{4,2},{6,4},{0,6},{3,1},{5,3},{7,5},{1,7},{10,8},{12,10},{14... | collective-permute-start | bytes 13736 | tf_op jit(solution)/shard_map/ppermute | solution.py:43
  13.8 14.3 %collective-permute-start.4 = (f32[286,2,2]{2,0,1:T(8,128)S(1)}, f32[286,2,2]{2,0,1:T(8,128)S(1)}, u32[]{:S(2)}, u32[]{:S(2)}) collective-permute-start(f32[286,2,2]{2,0,1:T(8,128)S(1)} %get-tuple-element.36), channel_id=1, source_target_pairs={{0,2},{2,4},{4,6},{6,0},{1,3},{3,5},{5,7},{7,1},{8,10},{10,12},{12... | collective-permute-start | bytes 13736 | tf_op jit(solution)/shard_map/ppermute | solution.py:43
  33.5 2.6 %copy-start = (f32[512,776]{0,1:T(8,128)}, f32[512,776]{0,1:T(8,128)S(1)}, u32[]{:S(2)}) copy-start(f32[512,776]{0,1:T(8,128)S(1)} %fusion.65) | copy-start | bytes 4767748
  36.1 9.2 %collective-permute-start.1 = (f32[512,2,1]{0,2,1:T(1,128)S(1)}, f32[512,2,1]{0,2,1:T(1,128)S(1)}, u32[]{:S(2)}, u32[]{:S(2)}) collective-permute-start(f32[512,2,1]{0,2,1:T(1,128)S(1)} %copy.97), channel_id=1, source_target_pairs={{2,0},{4,2},{6,4},{0,6},{3,1},{5,3},{7,5},{1,7},{10,8},{12,10},{14... | collective-permute-start | bytes 12296 | tf_op jit(solution)/shard_map/ppermute | solution.py:43
  37.6 11.7 %slice-start = ((f32[512,776]{0,1:T(8,128)}), f32[512,128]{0,1:T(8,128)S(1)}, s32[]{:S(2)}) async-start(f32[512,776]{0,1:T(8,128)} %copy-done), calls=%async_computation.1 | async-start | bytes 524288 | tf_op jit(solution)/shard_map/slice | solution.py:79
  37.6 12.3 %copy-start.1 = (f32[512,776]{0,1:T(8,128)S(1)}, f32[512,776]{0,1:T(8,128)}, u32[]{:S(2)}) copy-start(f32[512,776]{0,1:T(8,128)} %copy-done) | copy-start | bytes 4767748
  40.9 8.9 %collective-permute-start.6 = (f32[512,128]{0,1:T(8,128)S(1)}, f32[512,128]{0,1:T(8,128)}, u32[]{:S(2)}, u32[]{:S(2)}) collective-permute-start(f32[512,128]{0,1:T(8,128)S(1)} %bitcast.71), channel_id=1, source_target_pairs={{0,1},{1,8},{8,9},{9,16},{16,17},{17,24},{24,25},{25,0},{2,3},{3,1... | collective-permute-start | bytes 786440 | tf_op jit(solution)/shard_map/ppermute | solution.py:43
  41.0 10.1 %collective-permute-start.7 = (f32[512,128]{0,1:T(8,128)S(1)}, f32[512,128]{0,1:T(8,128)}, u32[]{:S(2)}, u32[]{:S(2)}) collective-permute-start(f32[512,128]{0,1:T(8,128)S(1)} %bitcast.68), channel_id=1, source_target_pairs={{1,0},{8,1},{9,8},{16,9},{17,16},{24,17},{25,24},{0,25},{3,2},{10,... | collective-permute-start | bytes 786440 | tf_op jit(solution)/shard_map/ppermute | solution.py:43
  44.7 4.5 %collective-permute-start = (f32[512,2,1]{0,2,1:T(1,128)S(1)}, f32[512,2,1]{0,2,1:T(1,128)S(1)}, u32[]{:S(2)}, u32[]{:S(2)}) collective-permute-start(f32[512,2,1]{0,2,1:T(1,128)S(1)} %copy.95), channel_id=1, source_target_pairs={{0,2},{2,4},{4,6},{6,0},{1,3},{3,5},{5,7},{7,1},{8,10},{10,12},{12... | collective-permute-start | bytes 12296 | tf_op jit(solution)/shard_map/ppermute | solution.py:43
  45.3 4.0 %copy-start.11 = (f32[512,1]{0,1:T(1,128)}, f32[512,1]{0,1:T(1,128)S(1)}, u32[]{:S(2)}) copy-start(f32[512,1]{0,1:T(1,128)S(1)} %get-tuple-element.47) | copy-start | bytes 6148
  45.3 5.7 %copy-start.7 = (f32[512,1]{0,1:T(1,128)}, f32[512,1]{0,1:T(1,128)S(1)}, u32[]{:S(2)}) copy-start(f32[512,1]{0,1:T(1,128)S(1)} %get-tuple-element.48) | copy-start | bytes 6148
  49.2 0.6 copy-start.13
  49.2 1.8 %copy-start.9 = (f32[512,1]{0,1:T(1,128)}, f32[512,1]{0,1:T(1,128)S(1)}, u32[]{:S(2)}) copy-start(f32[512,1]{0,1:T(1,128)S(1)} %get-tuple-element.46) | copy-start | bytes 6148
  51.0 1.3 %copy-start.5 = (f32[512]{0:T(512)S(1)}, f32[512]{0:T(512)}, u32[]{:S(2)}) copy-start(f32[512]{0:T(512)} %broadcast_divide_fusion) | copy-start | bytes 6148
  51.1 2.1 %copy-start.2 = (f32[286,2,128]{2,1,0:T(2,128)S(1)}, f32[286,2,128]{2,1,0:T(2,128)}, u32[]{:S(2)}) copy-start(f32[286,2,128]{2,1,0:T(2,128)} %param.7) | copy-start | bytes 878596
  51.1 2.1 %copy-start.3 = (f32[286,2,128]{2,1,0:T(2,128)S(1)}, f32[286,2,128]{2,1,0:T(2,128)}, u32[]{:S(2)}) copy-start(f32[286,2,128]{2,1,0:T(2,128)} %param.8) | copy-start | bytes 878596
  53.4 9.9 %collective-permute-start.11 = (f32[286,2,2]{2,0,1:T(8,128)S(1)}, f32[286,2,2]{2,0,1:T(8,128)S(1)}, u32[]{:S(2)}, u32[]{:S(2)}) collective-permute-start(f32[286,2,2]{2,0,1:T(8,128)S(1)} %get-tuple-element.23), channel_id=1, source_target_pairs={{2,0},{4,2},{6,4},{0,6},{3,1},{5,3},{7,5},{1,7},{10,8},{12,10},{14... | collective-permute-start | bytes 13736 | tf_op jit(solution)/shard_map/ppermute | solution.py:43
  53.5 16.9 %collective-permute-start.9 = (f32[286,2,128]{2,0,1:T(8,128)S(1)}, f32[286,2,128]{2,0,1:T(8,128)S(1)}, u32[]{:S(2)}, u32[]{:S(2)}) collective-permute-start(f32[286,2,128]{2,0,1:T(8,128)S(1)} %fusion.15), channel_id=1, source_target_pairs={{1,0},{8,1},{9,8},{16,9},{17,16},{24,17},{25,24},{0,25},{3,2},{10,... | collective-permute-start | bytes 878600 | tf_op jit(solution)/shard_map/ppermute | solution.py:43
  55.7 15.5 %collective-permute-start.8 = (f32[286,2,128]{2,0,1:T(8,128)S(1)}, f32[286,2,128]{2,0,1:T(8,128)S(1)}, u32[]{:S(2)}, u32[]{:S(2)}) collective-permute-start(f32[286,2,128]{2,0,1:T(8,128)S(1)} %fusion.15), channel_id=1, source_target_pairs={{0,1},{1,8},{8,9},{9,16},{16,17},{17,24},{24,25},{25,0},{2,3},{3,1... | collective-permute-start | bytes 878600 | tf_op jit(solution)/shard_map/ppermute | solution.py:43
  55.7 14.1 %collective-permute-start.10 = (f32[286,2,2]{2,0,1:T(8,128)S(1)}, f32[286,2,2]{2,0,1:T(8,128)S(1)}, u32[]{:S(2)}, u32[]{:S(2)}) collective-permute-start(f32[286,2,2]{2,0,1:T(8,128)S(1)} %get-tuple-element.24), channel_id=1, source_target_pairs={{0,2},{2,4},{4,6},{6,0},{1,3},{3,5},{5,7},{7,1},{8,10},{10,12},{12... | collective-permute-start | bytes 13736 | tf_op jit(solution)/shard_map/ppermute | solution.py:43
  73.3 2.8 %copy-start.12 = (f32[512,1]{0,1:T(1,128)S(1)}, f32[512,1]{0,1:T(1,128)}, u32[]{:S(2)}) copy-start(f32[512,1]{0,1:T(1,128)} %copy-done.11) | copy-start | bytes 6148
  73.3 2.8 %copy-start.14 = (f32[512,1]{0,1:T(1,128)S(1)}, f32[512,1]{0,1:T(1,128)}, u32[]{:S(2)}) copy-start(f32[512,1]{0,1:T(1,128)} %copy-done.13) | copy-start | bytes 6148
  76.1 1.3 %copy-start.8 = (f32[512,1]{0,1:T(1,128)S(1)}, f32[512,1]{0,1:T(1,128)}, u32[]{:S(2)}) copy-start(f32[512,1]{0,1:T(1,128)} %copy-done.7) | copy-start | bytes 6148
  76.1 1.3 %copy-start.10 = (f32[512,1]{0,1:T(1,128)S(1)}, f32[512,1]{0,1:T(1,128)}, u32[]{:S(2)}) copy-start(f32[512,1]{0,1:T(1,128)} %copy-done.9) | copy-start | bytes 6148
  77.4 1.2 %copy-start.6 = (f32[512]{0:T(512)S(1)}, f32[512]{0:T(512)}, u32[]{:S(2)}) copy-start(f32[512]{0:T(512)} %broadcast_divide_fusion) | copy-start | bytes 6148
where the time goes:
time: 81.1 us; the launch traced here: 80.5 us
  waiting for transfers between devices  25.1 us (31%)
  starting transfers between devices  20 us (25%)
  local copies, waits for them, and re-layouts  16.1 us (20%)
  matrix products  11.6 us (14%)
  other arithmetic  7.13 us (9%)
    ppermute x12, waiting for transfers between devices, shift_pair(): return (lax.ppermute(high, axis, up), lax.ppermute(low, axis, down))  25.1 us
    ppermute x12, starting transfers between devices, shift_pair(): return (lax.ppermute(high, axis, up), lax.ppermute(low, axis, down))  16.4 us
    unnamed x40, local copies, waits for them, and re-layouts  7.13 us
    dot_general x2, matrix products, local(): jnp.dot(chaos_basis, jnp.concatenate(parts + edges, 1), precision=top_pre...  6.67 us
    add x4, other arithmetic, local(): (flux_x[:, 2:] - flux_x[:, :-2]) * 0.5 + (flux_y[r + 2] - flux_y[r]) * 0.5  4.61 us
    all_to_all x1, starting transfers between devices, local(): lax.all_to_all(coef_points, 'chaos', split_axis=1, concat_axis=0, tiled=T...  3.6 us
    dot_general x1, matrix products, tables(): factors = jnp.einsum('qdn,pdn->qpd', at_nodes, mode_hot, precision=top_prec)  3.4 us
    concatenate x2, local copies, waits for them, and re-layouts, local(): jnp.concatenate(parts + edges, 1)  2.57 us
  transfers between devices with their start and end apart: 13, of which 5 were waited for; matrix products, arithmetic and copies ran while one was open for 24% of the time, Pallas kernels for 0%

commit v1 on v0

--- a/solution.py
+++ b/solution.py
@@ -10,6 +10,22 @@
 mass_shift = 1.0
 relax_rate = 0.2
 top_prec = lax.Precision.HIGHEST
+
+
+def exchange_in_pairs(shard, axis, split, join):
+    ways, here = (lax.axis_size(axis), lax.axis_index(axis))
+    width = shard.shape[split] // ways
+    lengths = list(shard.shape)
+    lengths[split] = width
+    height = lengths[join]
+    lengths[join] = height * ways
+    full = jnp.zeros(lengths, shard.dtype)
+    for mask in range(ways):
+        part = lax.dynamic_slice_in_dim(shard, (here ^ mask) * width, width, axis=split)
+        if mask:
+            part = lax.ppermute(part, axis, [(d, d ^ mask) for d in range(ways)])
+        full = lax.dynamic_update_slice_in_dim(full, part, (here ^ mask) * height, axis=join)
+    return full
 
 
 def tables(quad_index, mode_index):
@@ -51,7 +67,7 @@
     row_devs = lax.axis_size(rows)
     keep_low = jnp.where(row_dev == 0, 0.0, 1.0).astype(jnp.float32)
     keep_high = jnp.where(row_dev == row_devs - 1, 0.0, 1.0).astype(jnp.float32)
-    coef = lax.all_to_all(coef_points, "chaos", split_axis=1, concat_axis=0, tiled=True)
+    coef = exchange_in_pairs(coef_points, "chaos", 1, 0)
     coef = coef.reshape(points, row_len, col_len)
     k_low, k_high = shift_pair(coef[:, 0], coef[:, -1], rows)
     k_left, k_right = shift_pair(coef[:, :, :1], coef[:, :, -1:], "gx")

time: 81.1 us -> 77.7 us (0.958)
  other arithmetic: 7.13 us -> 4.62 us
  matrix products: 11.6 us -> 9.62 us
  waiting for transfers between devices: 25.1 us -> 27 us
  local copies, waits for them, and re-layouts: 16.1 us -> 15.2 us
    ppermute x0 -> x3, waiting for transfers between devices: none -> 5.61 us  [exchange_in_pairs(): part = lax.ppermute(part, axis, [(d, d ^ mask) for d in range(ways)])]
    unnamed x40 -> x20, local copies, waits for them, and re-layouts: 7.13 us -> 2.52 us
    add x4 -> x2, other arithmetic: 4.61 us -> 0.77 us  [local(): (flux_x[:, 2:] - flux_x[:, :-2]) * 0.5 + (flux_y[r + 2] - flux_y[r]) * 0.5]
    ppermute x12, waiting for transfers between devices: 25.1 us -> 21.4 us  [shift_pair(): return (lax.ppermute(high, axis, up), lax.ppermute(low, axis, down))]
    all_to_all x1 -> x0, starting transfers between devices: 3.6 us -> none  [local(): lax.all_to_all(coef_points, 'chaos', split_axis=1, concat_axis=0, tiled=T...]
    ppermute x0 -> x3, starting transfers between devices: none -> 2.92 us  [exchange_in_pairs(): part = lax.ppermute(part, axis, [(d, d ^ mask) for d in range(ways)])]
    squeeze x2, local copies, waits for them, and re-layouts: 0.04 us -> 1.47 us  [local(): v_right[:, r]]
    slice x1, local copies, waits for them, and re-layouts: 1.36 us -> 0.01 us  [local(): k_left, k_right = shift_pair(coef[:, :, :1], coef[:, :, -1:], 'gx')]
  transfers between devices with their start and end apart: 13 -> 15, of which waited for: 5 -> 7; matrix products, arithmetic and copies ran while one was open for 24% -> 24% of each run, Pallas kernels for 0% -> 0%
where the time goes in v1:
time: 77.7 us; the launch traced here: 77.3 us
  waiting for transfers between devices  27 us (35%)
  starting transfers between devices  20.4 us (26%)
  local copies, waits for them, and re-layouts  15.2 us (20%)
  matrix products  9.62 us (12%)
  other arithmetic  4.62 us (6%)
    ppermute x12, waiting for transfers between devices, shift_pair(): return (lax.ppermute(high, axis, up), lax.ppermute(low, axis, down))  21.4 us
    ppermute x12, starting transfers between devices, shift_pair(): return (lax.ppermute(high, axis, up), lax.ppermute(low, axis, down))  17.5 us
    ppermute x3, waiting for transfers between devices, exchange_in_pairs(): part = lax.ppermute(part, axis, [(d, d ^ mask) for d in range(ways)])  5.61 us
    dot_general x2, matrix products, local(): jnp.dot(chaos_basis, jnp.concatenate(parts + edges, 1), precision=top_pre...  5.45 us
    concatenate x2, local copies, waits for them, and re-layouts, local(): jnp.concatenate(parts + edges, 1)  3.07 us
    ppermute x3, starting transfers between devices, exchange_in_pairs(): part = lax.ppermute(part, axis, [(d, d ^ mask) for d in range(ways)])  2.92 us
    dot_general x1, matrix products, tables(): factors = jnp.einsum('qdn,pdn->qpd', at_nodes, mode_hot, precision=top_prec)  2.62 us
    unnamed x20, local copies, waits for them, and re-layouts  2.52 us
  transfers between devices with their start and end apart: 15, of which 7 were waited for; matrix products, arithmetic and copies ran while one was open for 24% of the time, Pallas kernels for 0%

profile of v1, /device:TPU:0, one launch (start us, length us, event | category | flops | bytes accessed | tf_op | source)
XLA Modules:
  0.0 77.3 jit_solution(10257930722334462012)
XLA Ops:
  0.0 1.0 %copy.63 = f32[286,2,128]{2,0,1:T(8,128)S(1)} copy(f32[286,2,128]{2,1,0:T(2,128)} %param.7) | data formatting | bytes 585728 | tf_op args[0]
  1.0 4.5 %collective-permute-start.6 = (f32[286,2,128]{2,0,1:T(8,128)S(1)}, f32[286,2,128]{2,0,1:T(8,128)}, u32[]{:S(2)}, u32[]{:S(2)}) collective-permute-start(f32[286,2,128]{2,0,1:T(8,128)S(1)} %copy.63), channel_id=1, source_target_pairs={{1,0},{8,1},{9,8},{16,9},{17,16},{24,17},{25,24},{0,25},{3,2},{10,... | collective-permute-start | bytes 878600 | tf_op jit(solution)/shard_map/ppermute | solution.py:59
  5.5 1.2 %constant_dynamic-slice_fusion = (f32[128,1,2,128]{3,2,1,0:T(2,128)S(1)}, f32[128,1,2,128]{3,2,1,0:T(2,128)S(1)}, f32[128,1,2,128]{3,2,1,0:T(2,128)S(1)}, f32[128,1,2,128]{3,2,1,0:T(2,128)S(1)}) fusion(f32[128,4,2,128]{3,2,1,0:T(2,128)} %param.9, s32[]{:T(128)S(6)} %select_n.37, s32[]{:T(128)S(6)} %select_n.35, s32[]{:T(128)S(6)} %select_n.33, s32[]{:T(128)S(6)} %select_n.31), kind=kLoop, calls=%fused_computation.115 | loop fusion | bytes 1048592 | tf_op jit(solution)/shard_map/dynamic_slice | solution.py:24
  6.7 0.1 copy.79
  6.8 0.1 collective-permute-start
  6.9 0.1 copy.80
  7.0 0.0 copy-start.7
  7.0 1.7 %collective-permute-start.1 = (f32[128,1,2,128]{0,3,2,1:T(8,128)S(1)}, f32[128,1,2,128]{0,3,2,1:T(8,128)S(1)}, u32[]{:S(2)}, u32[]{:S(2)}) collective-permute-start(f32[128,1,2,128]{0,3,2,1:T(8,128)S(1)} %copy.80), channel_id=1, source_target_pairs={{0,16},{8,24},{16,0},{24,8},{1,17},{9,25},{17,1},{25,9},{2,18},{10... | collective-permute-start | bytes 393224 | tf_op jit(solution)/shard_map/ppermute | solution.py:26
  8.7 0.1 fusion.65
  8.8 2.5 %collective-permute-start.8 = (f32[286,2,2]{2,0,1:T(8,128)S(1)}, f32[286,2,2]{2,0,1:T(8,128)S(1)}, u32[]{:S(2)}, u32[]{:S(2)}) collective-permute-start(f32[286,2,2]{2,0,1:T(8,128)S(1)} %get-tuple-element.43), channel_id=1, source_target_pairs={{2,0},{4,2},{6,4},{0,6},{3,1},{5,3},{7,5},{1,7},{10,8},{12,10},{14... | collective-permute-start | bytes 13736 | tf_op jit(solution)/shard_map/ppermute | solution.py:59
  11.4 0.1 select_reduce_fusion
  11.5 0.6 reduce_sum.19
  12.1 0.6 broadcast_divide_fusion
  12.8 0.2 fusion.54
  13.0 0.1 copy.50
  13.1 0.1 reshape.31
  13.2 2.6 %convolution_reduce_fusion = f32[286,512]{1,0:T(8,128)S(1)} fusion(f32[512,10,4]{0,2,1:T(4,128)S(1)} %fusion.54, s32[286,10]{0,1:T(8,128)S(1)} %copy-done.7), kind=kOutput, calls=%fused_computation | convolution fusion | flops 71616688 | bytes 679088 | tf_op jit(solution)/shard_map/qdn,pdn->qpd/dot_general | solution.py:47
  15.9 0.1 copy.81
  16.0 1.4 %collective-permute-done.8 = f32[286,2,2]{2,0,1:T(8,128)S(1)} collective-permute-done((f32[286,2,2]{2,0,1:T(8,128)S(1)}, f32[286,2,2]{2,0,1:T(8,128)S(1)}, u32[]{:S(2)}, u32[]{:S(2)}) %collective-permute-start.8) | collective-permute-done | bytes 4608 | tf_op jit(solution)/shard_map/ppermute | solution.py:59
  17.4 2.4 %collective-permute-start.7 = (f32[286,2,2]{2,0,1:T(8,128)S(1)}, f32[286,2,2]{2,0,1:T(8,128)S(1)}, u32[]{:S(2)}, u32[]{:S(2)}) collective-permute-start(f32[286,2,2]{2,0,1:T(8,128)S(1)} %get-tuple-element.44), channel_id=1, source_target_pairs={{0,2},{2,4},{4,6},{6,0},{1,3},{3,5},{5,7},{7,1},{8,10},{10,12},{12... | collective-permute-start | bytes 13736 | tf_op jit(solution)/shard_map/ppermute | solution.py:59
  19.8 0.7 slice_bitcast_fusion.12
  20.5 7.6 %collective-permute-done.7 = f32[286,2,2]{2,0,1:T(8,128)S(1)} collective-permute-done((f32[286,2,2]{2,0,1:T(8,128)S(1)}, f32[286,2,2]{2,0,1:T(8,128)S(1)}, u32[]{:S(2)}, u32[]{:S(2)}) %collective-permute-start.7) | collective-permute-done | bytes 4608 | tf_op jit(solution)/shard_map/ppermute | solution.py:59
  28.2 1.2 %collective-permute-start.2 = (f32[128,1,2,128]{0,3,2,1:T(8,128)S(1)}, f32[128,1,2,128]{0,3,2,1:T(8,128)S(1)}, u32[]{:S(2)}, u32[]{:S(2)}) collective-permute-start(f32[128,1,2,128]{0,3,2,1:T(8,128)S(1)} %copy.81), channel_id=1, source_target_pairs={{0,24},{8,16},{16,8},{24,0},{1,25},{9,17},{17,9},{25,1},{2,26},{10... | collective-permute-start | bytes 393224 | tf_op jit(solution)/shard_map/ppermute | solution.py:26
  29.3 0.7 slice_bitcast_fusion.14
  30.1 5.6 %collective-permute-done.2 = f32[128,1,2,128]{0,3,2,1:T(8,128)S(1)} collective-permute-done((f32[128,1,2,128]{0,3,2,1:T(8,128)S(1)}, f32[128,1,2,128]{0,3,2,1:T(8,128)S(1)}, u32[]{:S(2)}, u32[]{:S(2)}) %collective-permute-start.2) | collective-permute-done | bytes 131104 | tf_op jit(solution)/shard_map/ppermute | solution.py:26
  35.8 1.2 %collective-permute-start.3 = (f32[512,2,1]{0,2,1:T(1,128)S(1)}, f32[512,2,1]{0,2,1:T(1,128)S(1)}, u32[]{:S(2)}, u32[]{:S(2)}) collective-permute-start(f32[512,2,1]{0,2,1:T(1,128)S(1)} %get-tuple-element.23), channel_id=1, source_target_pairs={{0,2},{2,4},{4,6},{6,0},{1,3},{3,5},{5,7},{7,1},{8,10},{10,12},{12... | collective-permute-start | bytes 12296 | tf_op jit(solution)/shard_map/ppermute | solution.py:59
  37.0 1.9 %collective-permute-start.4 = (f32[512,2,1]{0,2,1:T(1,128)S(1)}, f32[512,2,1]{0,2,1:T(1,128)S(1)}, u32[]{:S(2)}, u32[]{:S(2)}) collective-permute-start(f32[512,2,1]{0,2,1:T(1,128)S(1)} %get-tuple-element.24), channel_id=1, source_target_pairs={{2,0},{4,2},{6,4},{0,6},{3,1},{5,3},{7,5},{1,7},{10,8},{12,10},{14... | collective-permute-start | bytes 12296 | tf_op jit(solution)/shard_map/ppermute | solution.py:59
  38.8 1.5 %collective-permute-done.3 = f32[512,2,1]{0,2,1:T(1,128)S(1)} collective-permute-done((f32[512,2,1]{0,2,1:T(1,128)S(1)}, f32[512,2,1]{0,2,1:T(1,128)S(1)}, u32[]{:S(2)}, u32[]{:S(2)}) %collective-permute-start.3) | collective-permute-done | bytes 4128 | tf_op jit(solution)/shard_map/ppermute | solution.py:59
  40.3 0.3 collective-permute-done.4
  40.6 1.0 %broadcast_multiply_fusion.1 = f32[286,2,128]{2,0,1:T(8,128)S(1)} fusion(f32[286,2,128]{2,0,1:T(8,128)} %collective-permute-done.6, f32[]{:T(128)S(6)} %select_n.40), kind=kLoop, calls=%fused_computation.98 | loop fusion | flops 73216 | bytes 585732 | tf_op jit(solution)/shard_map/mul | solution.py:82
  41.6 0.7 slice_bitcast_fusion.16
  42.4 1.0 %broadcast_multiply_fusion.3 = f32[286,2,128]{2,0,1:T(8,128)S(1)} fusion(f32[286,2,128]{2,0,1:T(8,128)} %collective-permute-done.5, f32[]{:T(128)S(6)} %select_n.39), kind=kLoop, calls=%fused_computation.100 | loop fusion | flops 73216 | bytes 585732 | tf_op jit(solution)/shard_map/mul | solution.py:81
  43.3 0.7 slice_bitcast_fusion.20
  44.1 1.5 %concatenate.47 = f32[286,776]{1,0:T(8,128)S(1)} concatenate(f32[286,128]{1,0:T(8,128)} %get-tuple-element.52, f32[286,128]{1,0:T(8,128)} %get-tuple-element.51, f32[286,128]{1,0:T(8,128)S(1)} %get-tuple-element.50, f32[286,128]{1,0:T(8,128)S(1)} %get-tuple-element.49, f32[286,128]{1,0:T(8,128)} %get-tuple-element.48, f32[286,128]{1,0:T(8,128)} %get-tuple-element.47, ...), dimensions={1} | concatenate | bytes 1775488 | tf_op jit(solution)/shard_map/concatenate | solution.py:91
  45.6 2.7 %fusion.66 = f32[512,776]{0,1:T(8,128)S(1)} fusion(f32[286,512]{1,0:T(8,128)S(1)} %convolution_reduce_fusion, f32[286,776]{1,0:T(8,128)S(1)} %concatenate.47), kind=kOutput, calls=%fused_computation.129 | convolution fusion | flops 1363574784 | bytes 3062720 | tf_op jit(solution)/shard_map/dot_general | solution.py:89
  48.3 0.2 fusion.19
  48.5 0.4 fusion.51
  48.9 0.3 copy-done.2
  49.2 0.7 fusion.2
  49.9 0.2 reshape.36
  50.1 0.1 copy-done
  50.2 0.1 copy-done.1
  50.3 0.1 fusion.15
  50.3 0.1 fusion.64
  50.5 2.8 %collective-permute-start.14 = (f32[286,2,2]{2,0,1:T(8,128)S(1)}, f32[286,2,2]{2,0,1:T(8,128)S(1)}, u32[]{:S(2)}, u32[]{:S(2)}) collective-permute-start(f32[286,2,2]{2,0,1:T(8,128)S(1)} %get-tuple-element.31), channel_id=1, source_target_pairs={{2,0},{4,2},{6,4},{0,6},{3,1},{5,3},{7,5},{1,7},{10,8},{12,10},{14... | collective-permute-start | bytes 13736 | tf_op jit(solution)/shard_map/ppermute | solution.py:59
  53.2 0.7 slice_bitcast_fusion.8
  54.0 1.4 %collective-permute-start.12 = (f32[286,2,128]{2,0,1:T(8,128)S(1)}, f32[286,2,128]{2,0,1:T(8,128)S(1)}, u32[]{:S(2)}, u32[]{:S(2)}) collective-permute-start(f32[286,2,128]{2,0,1:T(8,128)S(1)} %fusion.15), channel_id=1, source_target_pairs={{1,0},{8,1},{9,8},{16,9},{17,16},{24,17},{25,24},{0,25},{3,2},{10,... | collective-permute-start | bytes 878600 | tf_op jit(solution)/shard_map/ppermute | solution.py:59
  55.4 0.8 %collective-permute-start.13 = (f32[286,2,2]{2,0,1:T(8,128)S(1)}, f32[286,2,2]{2,0,1:T(8,128)S(1)}, u32[]{:S(2)}, u32[]{:S(2)}) collective-permute-start(f32[286,2,2]{2,0,1:T(8,128)S(1)} %get-tuple-element.32), channel_id=1, source_target_pairs={{0,2},{2,4},{4,6},{6,0},{1,3},{3,5},{5,7},{7,1},{8,10},{10,12},{12... | collective-permute-start | bytes 13736 | tf_op jit(solution)/shard_map/ppermute | solution.py:59
  56.3 4.5 %collective-permute-done.14 = f32[286,2,2]{2,0,1:T(8,128)S(1)} collective-permute-done((f32[286,2,2]{2,0,1:T(8,128)S(1)}, f32[286,2,2]{2,0,1:T(8,128)S(1)}, u32[]{:S(2)}, u32[]{:S(2)}) %collective-permute-start.14) | collective-permute-done | bytes 4608 | tf_op jit(solution)/shard_map/ppermute | solution.py:59
  60.8 0.7 slice_bitcast_fusion.2
  61.5 6.0 %collective-permute-done.13 = f32[286,2,2]{2,0,1:T(8,128)S(1)} collective-permute-done((f32[286,2,2]{2,0,1:T(8,128)S(1)}, f32[286,2,2]{2,0,1:T(8,128)S(1)}, u32[]{:S(2)}, u32[]{:S(2)}) %collective-permute-start.13) | collective-permute-done | bytes 4608 | tf_op jit(solution)/shard_map/ppermute | solution.py:59
  67.5 0.7 slice_bitcast_fusion.4
  68.3 0.7 slice_bitcast_fusion.6
  69.1 0.7 slice_bitcast_fusion.10
  69.8 1.6 %concatenate.54 = f32[286,776]{1,0:T(8,128)S(1)} concatenate(f32[286,128]{1,0:T(8,128)} %get-tuple-element.40, f32[286,128]{1,0:T(8,128)} %get-tuple-element.39, f32[286,128]{1,0:T(8,128)} %get-tuple-element.38, f32[286,128]{1,0:T(8,128)} %get-tuple-element.37, f32[286,128]{1,0:T(8,128)} %get-tuple-element.36, f32[286,128]{1,0:T(8,128)} %get-tuple-element.35, ...), dimensions={1} | concatenate | bytes 1775488 | tf_op jit(solution)/shard_map/concatenate | solution.py:91
  71.4 2.7 %fusion.67 = f32[512,776]{0,1:T(8,128)S(1)} fusion(f32[286,512]{1,0:T(8,128)S(1)} %convolution_reduce_fusion, f32[286,776]{1,0:T(8,128)S(1)} %concatenate.54), kind=kOutput, calls=%fused_computation.130 | convolution fusion | flops 1363574784 | bytes 3062720 | tf_op jit(solution)/shard_map/dot_general | solution.py:89
  74.2 0.1 fusion.23
  74.3 0.1 fusion.25
  74.4 0.7 copy-done.3
  75.1 0.4 fusion.37
  75.5 0.7 fusion
  76.1 0.2 reshape.37
  76.3 0.1 fusion.12
  76.4 0.9 %copy.74 = f32[286,2,128]{2,1,0:T(2,128)} copy(f32[286,2,128]{2,0,1:T(8,128)S(1)} %fusion.12) | data formatting | bytes 585728 | tf_op jit(solution)/shard_map/add | solution.py:113
  (39 shorter events, 0.3 us)
Async XLA Ops:
  1.0 39.7 %collective-permute-start.6 = (f32[286,2,128]{2,0,1:T(8,128)S(1)}, f32[286,2,128]{2,0,1:T(8,128)}, u32[]{:S(2)}, u32[]{:S(2)}) collective-permute-start(f32[286,2,128]{2,0,1:T(8,128)S(1)} %copy.63), channel_id=1, source_target_pairs={{1,0},{8,1},{9,8},{16,9},{17,16},{24,17},{25,24},{0,25},{3,2},{10,... | collective-permute-start | bytes 878600 | tf_op jit(solution)/shard_map/ppermute | solution.py:59
  5.5 36.8 %collective-permute-start.5 = (f32[286,2,128]{2,0,1:T(8,128)S(1)}, f32[286,2,128]{2,0,1:T(8,128)}, u32[]{:S(2)}, u32[]{:S(2)}) collective-permute-start(f32[286,2,128]{2,0,1:T(8,128)S(1)} %copy.63), channel_id=1, source_target_pairs={{0,1},{1,8},{8,9},{9,16},{16,17},{17,24},{24,25},{25,0},{2,3},{3,1... | collective-permute-start | bytes 878600 | tf_op jit(solution)/shard_map/ppermute | solution.py:59
  5.5 5.8 %copy-start.4 = (s32[512,10]{0,1:T(8,128)S(1)}, s32[512,10]{0,1:T(8,128)}, u32[]{:S(2)}) copy-start(s32[512,10]{0,1:T(8,128)} %param.10) | copy-start | bytes 61444
  5.5 5.8 %copy-start.6 = (f32[4]{0:T(128)S(1)}, f32[4]{0:T(128)}, u32[]{:S(2)}) copy-start(f32[4]{0:T(128)} %constant.57.clone) | copy-start | bytes 52
  5.5 7.3 %copy-start.5 = (f32[4,4,1]{1,0,2:T(4,128)S(1)}, f32[4,4,1]{1,0,2:T(4,128)}, u32[]{:S(2)}) copy-start(f32[4,4,1]{1,0,2:T(4,128)} %constant.71) | copy-start | bytes 196
  6.8 23.2 %collective-permute-start = (f32[128,1,2,128]{0,3,2,1:T(8,128)S(1)}, f32[128,1,2,128]{0,3,2,1:T(8,128)S(1)}, u32[]{:S(2)}, u32[]{:S(2)}) collective-permute-start(f32[128,1,2,128]{0,3,2,1:T(8,128)S(1)} %copy.79), channel_id=1, source_target_pairs={{0,8},{8,0},{16,24},{24,16},{1,9},{9,1},{17,25},{25,17},{2,10},{10... | collective-permute-start | bytes 393224 | tf_op jit(solution)/shard_map/ppermute | solution.py:26
  7.0 6.2 %copy-start.7 = (s32[286,10]{0,1:T(8,128)S(1)}, s32[286,10]{0,1:T(8,128)}, u32[]{:S(2)}) copy-start(s32[286,10]{0,1:T(8,128)} %param.11) | copy-start | bytes 34324
  7.0 23.1 %collective-permute-start.1 = (f32[128,1,2,128]{0,3,2,1:T(8,128)S(1)}, f32[128,1,2,128]{0,3,2,1:T(8,128)S(1)}, u32[]{:S(2)}, u32[]{:S(2)}) collective-permute-start(f32[128,1,2,128]{0,3,2,1:T(8,128)S(1)} %copy.80), channel_id=1, source_target_pairs={{0,16},{8,24},{16,0},{24,8},{1,17},{9,25},{17,1},{25,9},{2,18},{10... | collective-permute-start | bytes 393224 | tf_op jit(solution)/shard_map/ppermute | solution.py:26
  8.8 8.6 %collective-permute-start.8 = (f32[286,2,2]{2,0,1:T(8,128)S(1)}, f32[286,2,2]{2,0,1:T(8,128)S(1)}, u32[]{:S(2)}, u32[]{:S(2)}) collective-permute-start(f32[286,2,2]{2,0,1:T(8,128)S(1)} %get-tuple-element.43), channel_id=1, source_target_pairs={{2,0},{4,2},{6,4},{0,6},{3,1},{5,3},{7,5},{1,7},{10,8},{12,10},{14... | collective-permute-start | bytes 13736 | tf_op jit(solution)/shard_map/ppermute | solution.py:59
  17.4 10.8 %collective-permute-start.7 = (f32[286,2,2]{2,0,1:T(8,128)S(1)}, f32[286,2,2]{2,0,1:T(8,128)S(1)}, u32[]{:S(2)}, u32[]{:S(2)}) collective-permute-start(f32[286,2,2]{2,0,1:T(8,128)S(1)} %get-tuple-element.44), channel_id=1, source_target_pairs={{0,2},{2,4},{4,6},{6,0},{1,3},{3,5},{5,7},{7,1},{8,10},{10,12},{12... | collective-permute-start | bytes 13736 | tf_op jit(solution)/shard_map/ppermute | solution.py:59
  28.2 7.6 %collective-permute-start.2 = (f32[128,1,2,128]{0,3,2,1:T(8,128)S(1)}, f32[128,1,2,128]{0,3,2,1:T(8,128)S(1)}, u32[]{:S(2)}, u32[]{:S(2)}) collective-permute-start(f32[128,1,2,128]{0,3,2,1:T(8,128)S(1)} %copy.81), channel_id=1, source_target_pairs={{0,24},{8,16},{16,8},{24,0},{1,25},{9,17},{17,9},{25,1},{2,26},{10... | collective-permute-start | bytes 393224 | tf_op jit(solution)/shard_map/ppermute | solution.py:26
  35.8 4.6 %collective-permute-start.3 = (f32[512,2,1]{0,2,1:T(1,128)S(1)}, f32[512,2,1]{0,2,1:T(1,128)S(1)}, u32[]{:S(2)}, u32[]{:S(2)}) collective-permute-start(f32[512,2,1]{0,2,1:T(1,128)S(1)} %get-tuple-element.23), channel_id=1, source_target_pairs={{0,2},{2,4},{4,6},{6,0},{1,3},{3,5},{5,7},{7,1},{8,10},{10,12},{12... | collective-permute-start | bytes 12296 | tf_op jit(solution)/shard_map/ppermute | solution.py:59
  37.0 3.7 %collective-permute-start.4 = (f32[512,2,1]{0,2,1:T(1,128)S(1)}, f32[512,2,1]{0,2,1:T(1,128)S(1)}, u32[]{:S(2)}, u32[]{:S(2)}) collective-permute-start(f32[512,2,1]{0,2,1:T(1,128)S(1)} %get-tuple-element.24), channel_id=1, source_target_pairs={{2,0},{4,2},{6,4},{0,6},{3,1},{5,3},{7,5},{1,7},{10,8},{12,10},{14... | collective-permute-start | bytes 12296 | tf_op jit(solution)/shard_map/ppermute | solution.py:59
  38.8 9.7 %collective-permute-start.10 = (f32[512,128]{0,1:T(8,128)S(1)}, f32[512,128]{0,1:T(8,128)S(1)}, u32[]{:S(2)}, u32[]{:S(2)}) collective-permute-start(f32[512,128]{0,1:T(8,128)S(1)} %get-tuple-element.21), channel_id=1, source_target_pairs={{1,0},{8,1},{9,8},{16,9},{17,16},{24,17},{25,24},{0,25},{3,2},{10,... | collective-permute-start | bytes 786440 | tf_op jit(solution)/shard_map/ppermute | solution.py:59
  40.3 8.2 %collective-permute-start.9 = (f32[512,128]{0,1:T(8,128)S(1)}, f32[512,128]{0,1:T(8,128)S(1)}, u32[]{:S(2)}, u32[]{:S(2)}) collective-permute-start(f32[512,128]{0,1:T(8,128)S(1)} %get-tuple-element.22), channel_id=1, source_target_pairs={{0,1},{1,8},{8,9},{9,16},{16,17},{17,24},{24,25},{25,0},{2,3},{3,1... | collective-permute-start | bytes 786440 | tf_op jit(solution)/shard_map/ppermute | solution.py:59
  48.5 0.7 copy-start.2
  49.2 1.0 %copy-start = (f32[286,2,128]{2,1,0:T(2,128)S(1)}, f32[286,2,128]{2,1,0:T(2,128)}, u32[]{:S(2)}) copy-start(f32[286,2,128]{2,1,0:T(2,128)} %param.7) | copy-start | bytes 878596
  49.2 1.0 %copy-start.1 = (f32[286,2,128]{2,1,0:T(2,128)S(1)}, f32[286,2,128]{2,1,0:T(2,128)}, u32[]{:S(2)}) copy-start(f32[286,2,128]{2,1,0:T(2,128)} %param.8) | copy-start | bytes 878596
  50.5 10.3 %collective-permute-start.14 = (f32[286,2,2]{2,0,1:T(8,128)S(1)}, f32[286,2,2]{2,0,1:T(8,128)S(1)}, u32[]{:S(2)}, u32[]{:S(2)}) collective-permute-start(f32[286,2,2]{2,0,1:T(8,128)S(1)} %get-tuple-element.31), channel_id=1, source_target_pairs={{2,0},{4,2},{6,4},{0,6},{3,1},{5,3},{7,5},{1,7},{10,8},{12,10},{14... | collective-permute-start | bytes 13736 | tf_op jit(solution)/shard_map/ppermute | solution.py:59
  54.0 14.3 %collective-permute-start.12 = (f32[286,2,128]{2,0,1:T(8,128)S(1)}, f32[286,2,128]{2,0,1:T(8,128)S(1)}, u32[]{:S(2)}, u32[]{:S(2)}) collective-permute-start(f32[286,2,128]{2,0,1:T(8,128)S(1)} %fusion.15), channel_id=1, source_target_pairs={{1,0},{8,1},{9,8},{16,9},{17,16},{24,17},{25,24},{0,25},{3,2},{10,... | collective-permute-start | bytes 878600 | tf_op jit(solution)/shard_map/ppermute | solution.py:59
  55.4 13.6 %collective-permute-start.11 = (f32[286,2,128]{2,0,1:T(8,128)S(1)}, f32[286,2,128]{2,0,1:T(8,128)S(1)}, u32[]{:S(2)}, u32[]{:S(2)}) collective-permute-start(f32[286,2,128]{2,0,1:T(8,128)S(1)} %fusion.15), channel_id=1, source_target_pairs={{0,1},{1,8},{8,9},{9,16},{16,17},{17,24},{24,25},{25,0},{2,3},{3,1... | collective-permute-start | bytes 878600 | tf_op jit(solution)/shard_map/ppermute | solution.py:59
  55.4 12.1 %collective-permute-start.13 = (f32[286,2,2]{2,0,1:T(8,128)S(1)}, f32[286,2,2]{2,0,1:T(8,128)S(1)}, u32[]{:S(2)}, u32[]{:S(2)}) collective-permute-start(f32[286,2,2]{2,0,1:T(8,128)S(1)} %get-tuple-element.32), channel_id=1, source_target_pairs={{0,2},{2,4},{4,6},{6,0},{1,3},{3,5},{5,7},{7,1},{8,10},{10,12},{12... | collective-permute-start | bytes 13736 | tf_op jit(solution)/shard_map/ppermute | solution.py:59
  74.1 1.0 %copy-start.3 = (f32[512,128]{0,1:T(8,128)S(1)}, f32[512,128]{0,1:T(8,128)}, u32[]{:S(2)}) copy-start(f32[512,128]{0,1:T(8,128)} %copy-done.2) | copy-start | bytes 786436
